TPU v7x, 512 devices: a whole 4x8x8 slice. The times are simulated.
512 devices in a mesh: layer: 8 (over x, z_hi), row: 8 (over y), col: 8 (over z_lo, core).
Axes of the slice: x: 4, y: 8, z: 8 (z_hi: 2, z_lo: 4; z = z_hi * 4 + z_lo), core: 2. Of those that a mesh axis runs over, the one named last changes fastest.
Arguments:
- schur_window: float32 [4, 8, 256, 2, 8, 256], P(None, 'row', None, None, 'col'), may hold values from -8 to 24, as said below
Outputs:
- factored: float32 [4, 8, 256, 2, 8, 256], P(None, 'row', 'layer', None, 'col')
Inputs may be any that keep to these rules, and one draw needn't show every extreme that they name: `schur_window`: the leading 4096 columns of a symmetric positive definite matrix: its leading 4096 x 4096 block is symmetric and positive definite.
All inputs are finite; a program needn't handle non-finite values.
Results may differ from a plain program's by a relative error of at most 0.0001.
Values sent between devices are 32-bit elements; how exact they have to be, the bound alone decides.
No kernel may reach another device: no remote copies, remote signals or barrier semaphores. Data moves between devices by JAX's collectives and lax.ppermute only.
A program may use at most 64 MiB of HBM per device.

v0:
```python
import jax
import jax.numpy as jnp
from jax import lax
from jax.sharding import PartitionSpec as P

PANELS = 2


def picked(array, axis, root):
    return lax.dynamic_index_in_dim(lax.all_gather(array, axis), root, 0, keepdims=False)


def spread(array, axis, root):
    mine = lax.axis_index(axis) == root
    return lax.psum(jnp.where(mine, array, jnp.zeros_like(array)), axis)


def padded_to(lines, peers):
    spare = -len(lines) % peers
    return jnp.pad(lines, [(0, spare)] + [(0, 0)] * (lines.ndim - 1))


def broadcast_by_parts(array, axis, root):
    lines = jnp.where(lax.axis_index(axis) == root, array, jnp.zeros_like(array)).reshape(
        -1, *array.shape[1:][-1:]
    )
    padded = padded_to(lines, lax.axis_size(axis))
    own = lax.psum_scatter(padded, axis, scatter_dimension=0, tiled=True)
    return lax.all_gather(own, axis, axis=0, tiled=True)[: len(lines)].reshape(array.shape)


def in_blocks(array, dim, peers):
    before, after = (array.shape[:dim], array.shape[dim + 1 :])
    return jnp.moveaxis(array.reshape(*before, peers, -1, *after), dim, 0)


def sent_and_summed(array, axis, dim):
    peers = lax.axis_size(axis)
    pieces = lax.all_to_all(in_blocks(array, dim, peers), axis, 0, 0, tiled=True)
    return jnp.sum(pieces, axis=0)


def solve_rows(factor, column):
    block_count, panel_width, _ = column.shape
    flattened = column.reshape(block_count * panel_width, panel_width)
    solved = jax.scipy.linalg.solve_triangular(factor, flattened.T, lower=True)
    return solved.T.reshape(block_count, panel_width, panel_width)


def shape_panel(factor, solved, row_number, panel_index):
    row_marks = row_number[:, None, None]
    lower_rows = jnp.where(row_marks > panel_index, solved, jnp.zeros_like(solved))
    return jnp.where(row_marks == panel_index, factor[None], lower_rows)


def block_products(row_part, col_part):
    block_count, panel_width, _ = row_part.shape
    slot_count = col_part.shape[0]
    product = jnp.dot(
        row_part.reshape(block_count * panel_width, panel_width),
        col_part.reshape(slot_count * panel_width, panel_width).T,
        precision=lax.Precision.HIGHEST,
        preferred_element_type=jnp.float32,
    )
    return product.reshape(block_count, panel_width, slot_count, panel_width)


def add_slots(updates, row_part, col_part, active):

    def increase(current):
        return current + block_products(row_part, col_part)

    def unchanged(current):
        return current

    return lax.cond(active, increase, unchanged, updates)


def local(schur_window):
    row_blocks = schur_window.shape[0]
    panel_width = schur_window.shape[2]
    col_blocks = schur_window.shape[3]
    held_blocks = schur_window.reshape(row_blocks, panel_width, col_blocks, panel_width)
    grid_rows = lax.axis_size("row")
    grid_cols = lax.axis_size("col")
    layer_count = lax.axis_size("layer")
    layer_here = lax.axis_index("layer")
    col_here = lax.axis_index("col")
    row_number = jnp.arange(row_blocks, dtype=jnp.int32) * grid_rows + lax.axis_index("row")
    col_number = jnp.arange(col_blocks, dtype=jnp.int32) * grid_cols + col_here
    identity = jnp.eye(panel_width, dtype=jnp.float32)
    updates = jnp.zeros_like(held_blocks)
    for panel_index in range(PANELS):
        owner_col = panel_index % grid_cols
        owner_slot = panel_index // grid_cols
        pivot_row = panel_index % grid_rows
        pivot_slot = panel_index // grid_rows
        owner_layer = panel_index % layer_count
        column_here = held_blocks[:, :, owner_slot, :]
        if panel_index > 0:
            column_here = column_here - lax.psum(updates[:, :, owner_slot, :], "layer")
        pivot_here = column_here[pivot_slot]
        in_owner_col = col_here == owner_col
        pivot = picked(pivot_here, "row", pivot_row)
        factor = jnp.linalg.cholesky(jnp.where(in_owner_col, pivot, identity))
        panel_mine = shape_panel(factor, solve_rows(factor, column_here), row_number, panel_index)
        panel_rows = spread(panel_mine, "col", owner_col)
        pieces = []
        for col_slot in range(col_blocks):
            target = col_number[col_slot]
            source_slot = jnp.minimum(target // grid_rows, row_blocks - 1)
            piece = lax.dynamic_index_in_dim(panel_rows, source_slot, 0, keepdims=False)
            pieces.append(broadcast_by_parts(piece, "row", target % grid_rows))
        col_panel = jnp.stack(pieces)
        row_part = jnp.where(
            row_number[:, None, None] > panel_index, panel_rows, jnp.zeros_like(panel_rows)
        )
        col_part = jnp.where(
            col_number[:, None, None] > panel_index, col_panel, jnp.zeros_like(col_panel)
        )
        active = layer_here == owner_layer
        updates = add_slots(updates, row_part, col_part, active)
        kept_column = jnp.where(in_owner_col, panel_rows, held_blocks[:, :, owner_slot, :])
        held_blocks = held_blocks.at[:, :, owner_slot, :].set(kept_column)
    summed = sent_and_summed(updates, "layer", 1)
    share_rows = summed.shape[1]
    held_share = lax.dynamic_slice_in_dim(held_blocks, layer_here * share_rows, share_rows, 1)
    factored_cols = (col_number < PANELS)[None, None, :, None]
    upper_part = (row_number[:, None, None, None] < PANELS) & (
        col_number[None, None, :, None] > row_number[:, None, None, None]
    )
    result = jnp.where(factored_cols, held_share, held_share - summed)
    result = jnp.where(upper_part, jnp.zeros_like(result), result)
    return result.reshape(row_blocks, 1, share_rows, col_blocks, 1, panel_width)


def solution(mesh):
    return jax.shard_map(
        local,
        mesh=mesh,
        in_specs=(P(None, "row", None, None, "col", None),),
        out_specs=P(None, "row", "layer", None, "col", None),
        check_vma=False,
    )
```

profile of v0, /device:TPU:64, one launch (start us, length us, event | category | flops | bytes accessed | tf_op | source)
XLA Modules:
  0.0 830.7 jit_solution(384619336028586609)
XLA Ops:
  6.5 1.8 copy.102
  10.2 1.6 copy.68
  11.8 44.9 %all-gather.6.cloned.1.call-done = f32[8,256,1,256]{3,1,2,0:T(8,128)} async-done(((f32[1,256,1,256]{3,1,2,0:T(8,128)}), f32[8,256,1,256]{3,1,2,0:T(8,128)}) %all-gather.6.cloned.1.call-update) | async-done | bytes 2097168 | tf_op jit(solution)/shard_map/all_gather | solution.py:10
  58.1 11.7 %cholesky.130 = f32[128,128]{1,0:T(8,128)S(1)} custom-call(f32[128,128]{1,0:T(8,128)S(1)} %cholesky.194), custom_call_target="Cholesky" | custom-call | tf_op jit(solution)/shard_map/jit(cholesky)/cholesky | solution.py:105
  69.8 9.8 %custom-call.13 = f32[1,128,128]{1,2,0:T(8,128)S(1)} custom-call(f32[1,128,128]{2,1,0:T(8,128)S(1)} %get-tuple-element.173), custom_call_target="InvertDiagBlocksLowerTriangular" | custom-call | tf_op jit(solution)/shard_map/jit(cholesky)/cholesky | solution.py:105
  80.1 11.7 %cholesky.147 = f32[128,128]{1,0:T(8,128)S(1)} custom-call(f32[128,128]{1,0:T(8,128)S(1)} %convolution_subtract_fusion.3), custom_call_target="Cholesky" | custom-call | tf_op jit(solution)/shard_map/jit(cholesky)/cholesky | solution.py:105
  93.9 4.3 while.6
  94.9 1.3 bitcast_dynamic-update-slice_fusion.6
  96.8 1.3 bitcast_dynamic-update-slice_fusion.6
  98.7 19.7 %custom-call.14 = f32[2,128,128]{1,2,0:T(8,128)S(1)} custom-call(f32[2,128,128]{2,1,0:T(8,128)S(1)} %get-tuple-element.104), custom_call_target="InvertDiagBlocksLowerTriangular" | custom-call | tf_op jit(solution)/shard_map/jit(_solve_triangular)/triangular_solve | solution.py:46
  120.6 1.2 select_select_fusion.1
  127.3 71.2 %all-reduce.5.cloned.1.call-done = f32[4,256,256]{2,1,0:T(8,128)} async-done(((f32[4,256,256]{2,1,0:T(8,128)}), f32[4,256,256]{2,1,0:T(8,128)}) %all-reduce.5.cloned.1.call-update) | async-done | bytes 1048592 | tf_op jit(solution)/shard_map/psum | solution.py:15
  198.5 1.8 select_bitcast_fusion.3
  201.0 41.5 %reduce-scatter.13.cloned.1.call-done = f32[32,256]{1,0:T(8,128)} async-done(((f32[256,256]{1,0:T(8,128)}), f32[32,256]{1,0:T(8,128)}) %reduce-scatter.13.cloned.1.call-update) | async-done | bytes 32784 | tf_op jit(solution)/shard_map/reduce_scatter | solution.py:28
  242.5 25.0 %all_gather.19 = f32[256,256]{1,0:T(8,128)S(1)} all-gather(f32[32,256]{1,0:T(8,128)} %reduce-scatter.13.cloned.1.call-done), channel_id=1, replica_groups=mesh['layer'=8,'row'=8,'col'=8] {'row'}, dimensions={0}, use_global_device_ids=true | all-gather | bytes 294912 | tf_op jit(solution)/shard_map/all_gather | solution.py:29
  267.5 16.2 %reduce-scatter.15.cloned.1.call-done = f32[32,256]{1,0:T(8,128)} async-done(((f32[256,256]{1,0:T(8,128)}), f32[32,256]{1,0:T(8,128)}) %reduce-scatter.15.cloned.1.call-update) | async-done | bytes 32784 | tf_op jit(solution)/shard_map/reduce_scatter | solution.py:28
  283.7 25.0 %all_gather.20 = f32[256,256]{1,0:T(8,128)S(1)} all-gather(f32[32,256]{1,0:T(8,128)} %reduce-scatter.15.cloned.1.call-done), channel_id=1, replica_groups=mesh['layer'=8,'row'=8,'col'=8] {'row'}, dimensions={0}, use_global_device_ids=true | all-gather | bytes 294912 | tf_op jit(solution)/shard_map/all_gather | solution.py:29
  311.6 3.5 conditional.2
  311.6 3.5 fusion
  316.2 133.4 %all-reduce.7.cloned.1.call-done = f32[4,256,256]{2,1,0:T(8,128)} async-done(((f32[4,256,256]{2,1,0:T(8,128)}), f32[4,256,256]{2,1,0:T(8,128)}) %all-reduce.7.cloned.1.call-update) | async-done | bytes 1048592 | tf_op jit(solution)/shard_map/psum | solution.py:101
  449.6 1.8 fusion.31
  453.5 2.6 copy.77
  456.0 38.1 %all-gather.4.cloned.1.call-done = f32[8,256,256]{2,1,0:T(8,128)} async-done(((f32[1,256,256]{2,1,0:T(8,128)}), f32[8,256,256]{2,1,0:T(8,128)}) %all-gather.4.cloned.1.call-update) | async-done | bytes 2097168 | tf_op jit(solution)/shard_map/all_gather | solution.py:10
  494.2 1.7 dynamic_slice.30
  497.6 1.8 copy.76
  501.1 11.7 %cholesky.164 = f32[128,128]{1,0:T(8,128)S(1)} custom-call(f32[128,128]{1,0:T(8,128)S(1)} %cholesky.197), custom_call_target="Cholesky" | custom-call | tf_op jit(solution)/shard_map/jit(cholesky)/cholesky | solution.py:105
  512.9 9.8 %custom-call.15 = f32[1,128,128]{1,2,0:T(8,128)S(1)} custom-call(f32[1,128,128]{2,1,0:T(8,128)S(1)} %get-tuple-element.169), custom_call_target="InvertDiagBlocksLowerTriangular" | custom-call | tf_op jit(solution)/shard_map/jit(cholesky)/cholesky | solution.py:105
  524.9 11.7 %cholesky.181 = f32[128,128]{1,0:T(8,128)S(1)} custom-call(f32[128,128]{1,0:T(8,128)S(1)} %convolution_subtract_fusion.2), custom_call_target="Cholesky" | custom-call | tf_op jit(solution)/shard_map/jit(cholesky)/cholesky | solution.py:105
  539.1 1.7 fusion.19
  540.8 5.2 while.7
  542.3 1.3 bitcast_dynamic-update-slice_fusion.7
  544.8 1.3 bitcast_dynamic-update-slice_fusion.7
  546.7 20.5 %custom-call.16 = f32[2,128,128]{1,2,0:T(8,128)S(1)} custom-call(f32[2,128,128]{2,1,0:T(8,128)} %copy-done.8), custom_call_target="InvertDiagBlocksLowerTriangular" | custom-call | tf_op jit(solution)/shard_map/jit(_solve_triangular)/triangular_solve | solution.py:46
  567.2 1.7 fusion.11
  568.9 1.6 convolution_subtract_fusion
  572.2 2.5 copy.78
  574.8 2.4 select_select_fusion
  577.2 76.6 %all-reduce.9.cloned.1.call-done = f32[4,256,256]{2,1,0:T(8,128)} async-done(((f32[4,256,256]{2,1,0:T(8,128)}), f32[4,256,256]{2,1,0:T(8,128)}) %all-reduce.9.cloned.1.call-update) | async-done | bytes 1048592 | tf_op jit(solution)/shard_map/psum | solution.py:15
  653.8 1.9 select_bitcast_fusion.1
  656.5 41.3 %reduce-scatter.17.cloned.1.call-done = f32[32,256]{1,0:T(8,128)} async-done(((f32[256,256]{1,0:T(8,128)}), f32[32,256]{1,0:T(8,128)}) %reduce-scatter.17.cloned.1.call-update) | async-done | bytes 32784 | tf_op jit(solution)/shard_map/reduce_scatter | solution.py:28
  697.8 25.0 %all_gather.22 = f32[256,256]{1,0:T(8,128)S(1)} all-gather(f32[32,256]{1,0:T(8,128)} %reduce-scatter.17.cloned.1.call-done), channel_id=1, replica_groups=mesh['layer'=8,'row'=8,'col'=8] {'row'}, dimensions={0}, use_global_device_ids=true | all-gather | bytes 294912 | tf_op jit(solution)/shard_map/all_gather | solution.py:29
  722.8 16.4 %reduce-scatter.19.cloned.1.call-done = f32[32,256]{1,0:T(8,128)} async-done(((f32[256,256]{1,0:T(8,128)}), f32[32,256]{1,0:T(8,128)}) %reduce-scatter.19.cloned.1.call-update) | async-done | bytes 32784 | tf_op jit(solution)/shard_map/reduce_scatter | solution.py:28
  739.2 25.0 %all_gather.23 = f32[256,256]{1,0:T(8,128)S(1)} all-gather(f32[32,256]{1,0:T(8,128)} %reduce-scatter.19.cloned.1.call-done), channel_id=1, replica_groups=mesh['layer'=8,'row'=8,'col'=8] {'row'}, dimensions={0}, use_global_device_ids=true | all-gather | bytes 294912 | tf_op jit(solution)/shard_map/all_gather | solution.py:29
  765.2 1.5 copy.84
  766.7 10.9 %all-to-all-start = ((f32[8,4,32,2,256]{4,2,3,1,0:T(8,128)}), f32[8,4,32,2,256]{4,2,3,1,0:T(8,128)}, u32[]{:S(2)}, u32[]{:S(2)}) async-start(f32[8,4,32,2,256]{4,2,3,1,0:T(8,128)} %copy.84), calls=%async_computation | async-start | bytes 4194304 | tf_op jit(solution)/shard_map/all_to_all | solution.py:39
  777.8 1.6 copy.79
  780.5 39.6 %all-to-all-done = f32[8,4,32,2,256]{4,2,3,1,0:T(8,128)} async-done(((f32[8,4,32,2,256]{4,2,3,1,0:T(8,128)}), f32[8,4,32,2,256]{4,2,3,1,0:T(8,128)}, u32[]{:S(2)}, u32[]{:S(2)}) %all-to-all-start) | async-done | bytes 2097184 | tf_op jit(solution)/shard_map/all_to_all | solution.py:39
  820.1 1.8 reduce_sum.9
  (106 shorter events, 32.7 us)
Async XLA Ops:
  6.5 50.2 %all-gather.6.cloned.1.call-start = ((), (), s32[]{:S(2)}) async-start(), calls=%async_computation.9 | async-start | bytes 2359296 | tf_op jit(solution)/shard_map/all_gather | solution.py:10
  8.3 3.5 copy-start
  9.1 189.4 %all-reduce.5.cloned.1.call-start = ((), (), s32[]{:S(2)}) async-start(), calls=%async_computation.5 | async-start | bytes 2097152 | tf_op jit(solution)/shard_map/psum | solution.py:15
  98.1 0.5 copy-start.9
  121.9 120.6 %reduce-scatter.13.cloned.1.call-start = ((), (), s32[]{:S(2)}) async-start(), calls=%async_computation.10 | async-start | bytes 294912 | tf_op jit(solution)/shard_map/reduce_scatter | solution.py:28
  200.3 111.3 %copy-start.2 = (f32[4,256,256]{2,1,0:T(8,128)S(1)}, f32[4,256,256]{2,1,0:T(8,128)}, u32[]{:S(2)}) copy-start(f32[4,256,256]{2,1,0:T(8,128)} %all-reduce.5.cloned.1.call-done) | copy-start | bytes 3145732
  200.4 83.4 %reduce-scatter.15.cloned.1.call-start = ((), (), s32[]{:S(2)}) async-start(), calls=%async_computation.11 | async-start | bytes 294912 | tf_op jit(solution)/shard_map/reduce_scatter | solution.py:28
  201.0 248.7 %all-reduce.7.cloned.1.call-start = ((), (), s32[]{:S(2)}) async-start(), calls=%async_computation.6 | async-start | bytes 2097152 | tf_op jit(solution)/shard_map/psum | solution.py:101
  316.2 178.0 %all-gather.4.cloned.1.call-start = ((), (), s32[]{:S(2)}) async-start(), calls=%async_computation.7 | async-start | bytes 2359296 | tf_op jit(solution)/shard_map/all_gather | solution.py:10
  451.5 1.0 copy-start.4
  453.2 200.6 %all-reduce.9.cloned.1.call-start = ((), (), s32[]{:S(2)}) async-start(), calls=%async_computation.8 | async-start | bytes 2097152 | tf_op jit(solution)/shard_map/psum | solution.py:15
  500.4 0.7 copy-start.7
  536.6 2.5 copy-start.6
  546.1 0.6 copy-start.8
  571.2 3.6 copy-start.5
  577.2 120.6 %reduce-scatter.17.cloned.1.call-start = ((), (), s32[]{:S(2)}) async-start(), calls=%async_computation.12 | async-start | bytes 294912 | tf_op jit(solution)/shard_map/reduce_scatter | solution.py:28
  655.7 83.5 %reduce-scatter.19.cloned.1.call-start = ((), (), s32[]{:S(2)}) async-start(), calls=%async_computation.13 | async-start | bytes 294912 | tf_op jit(solution)/shard_map/reduce_scatter | solution.py:28
  766.7 11.0 %copy-start.1 = (f32[4,1,256,2,1,256]{5,2,0,3,4,1:T(8,128)S(1)}, f32[4,1,256,2,1,256]{5,2,0,3,4,1:T(8,128)}, u32[]{:S(2)}) copy-start(f32[4,1,256,2,1,256]{5,2,0,3,4,1:T(8,128)} %copy-done) | copy-start | bytes 6291460
  766.7 53.4 %all-to-all-start = ((f32[8,4,32,2,256]{4,2,3,1,0:T(8,128)}), f32[8,4,32,2,256]{4,2,3,1,0:T(8,128)}, u32[]{:S(2)}, u32[]{:S(2)}) async-start(f32[8,4,32,2,256]{4,2,3,1,0:T(8,128)} %copy.84), calls=%async_computation | async-start | bytes 4194304 | tf_op jit(solution)/shard_map/all_to_all | solution.py:39
  777.8 1.6 copy-start.3
Sparse Core Ops, SparseCore 0:
  9.4 47.2 all-gather.5
  122.0 76.4 all-reduce.4
  201.3 41.1 reduce-scatter.12
  245.1 38.5 reduce-scatter.14
  316.3 133.2 all-reduce.6
  453.3 40.7 all-gather.3
  577.3 76.4 all-reduce.8
  656.6 41.1 reduce-scatter.16
  700.6 38.5 reduce-scatter.18
where the time goes:
time: 840 us; the launch traced here: 831 us
  waiting for transfers between devices  521 us (62%)
  other arithmetic  128 us (15%)
  blocking collectives  100 us (12%)
  local copies, waits for them, and re-layouts  36.7 us (4%)
  between operations  21.1 us (3%)
  matrix products  11.8 us (1%)
  starting transfers between devices  11.4 us (1%)
    psum x2, waiting for transfers between devices, spread(): return lax.psum(jnp.where(mine, array, jnp.zeros_like(array)), axis)  148 us
    psum x1, waiting for transfers between devices, local(): column_here = column_here - lax.psum(updates[:, :, owner_slot, :], 'layer')  133 us
    reduce_scatter x4, waiting for transfers between devices, broadcast_by_parts(): own = lax.psum_scatter(padded, axis, scatter_dimension=0, tiled=True)  115 us
    all_gather x4, blocking collectives, broadcast_by_parts(): lax.all_gather(own, axis, axis=0, tiled=True)[:len(lines)]  100 us
    all_gather x2, waiting for transfers between devices, picked(): lax.all_gather(array, axis)  83 us
    another operation x13, other arithmetic, local(): factor = jnp.linalg.cholesky(jnp.where(in_owner_col, pivot, identity))  68.5 us
    another operation x5, other arithmetic, solve_rows(): solved = jax.scipy.linalg.solve_triangular(factor, flattened.T, lower=True)  41.9 us
    all_to_all x1, waiting for transfers between devices, sent_and_summed(): lax.all_to_all(in_blocks(array, dim, peers), axis, 0, 0, tiled=True)  39.6 us
  transfers between devices with their start and end apart: 10, of which 10 were waited for; matrix products, arithmetic and copies ran while one was open for 1% of the time, Pallas kernels for 0%

commit v1 on v0

--- a/solution.py
+++ b/solution.py
@@ -12,7 +12,7 @@
 
 def spread(array, axis, root):
     mine = lax.axis_index(axis) == root
-    return lax.psum(jnp.where(mine, array, jnp.zeros_like(array)), axis)
+    return jnp.sum(lax.all_gather(jnp.where(mine, array, jnp.zeros_like(array)), axis), axis=0)
 
 
 def padded_to(lines, peers):

time: 840 us -> 912 us (1.086)
  local copies, waits for them, and re-layouts: 36.7 us -> 63.4 us
  waiting for transfers between devices: 521 us -> 542 us
  other arithmetic: 128 us -> 144 us
    all_gather x0 -> x2, waiting for transfers between devices: none -> 176 us  [spread(): lax.all_gather(jnp.where(mine, array, jnp.zeros_like(array)), axis)]
    psum x2 -> x0, waiting for transfers between devices: 148 us -> none  [spread(): return lax.psum(jnp.where(mine, array, jnp.zeros_like(array)), axis)]
    unnamed x23 -> x29, local copies, waits for them, and re-layouts: 5.87 us -> 22.1 us
    reduce_sum x0 -> x2, other arithmetic: none -> 10.2 us  [spread(): jnp.sum(lax.all_gather(jnp.where(mine, array, jnp.zeros_like(array)), axi...]
  transfers between devices with their start and end apart: 10 -> 10, of which waited for: 10 -> 10; matrix products, arithmetic and copies ran while one was open for 1% -> 2% of each run, Pallas kernels for 0% -> 0%
where the time goes in v1:
time: 912 us; the launch traced here: 902 us
  waiting for transfers between devices  542 us (59%)
  other arithmetic  144 us (16%)
  blocking collectives  100 us (11%)
  local copies, waits for them, and re-layouts  63.4 us (7%)
  between operations  21.4 us (2%)
  matrix products  15.6 us (2%)
  starting transfers between devices  15.4 us (2%)
    all_gather x2, waiting for transfers between devices, spread(): lax.all_gather(jnp.where(mine, array, jnp.zeros_like(array)), axis)  176 us
    psum x1, waiting for transfers between devices, local(): column_here = column_here - lax.psum(updates[:, :, owner_slot, :], 'layer')  132 us
    reduce_scatter x4, waiting for transfers between devices, broadcast_by_parts(): own = lax.psum_scatter(padded, axis, scatter_dimension=0, tiled=True)  117 us
    all_gather x4, blocking collectives, broadcast_by_parts(): lax.all_gather(own, axis, axis=0, tiled=True)[:len(lines)]  100 us
    all_gather x2, waiting for transfers between devices, picked(): lax.all_gather(array, axis)  78.8 us
    another operation x13, other arithmetic, local(): factor = jnp.linalg.cholesky(jnp.where(in_owner_col, pivot, identity))  68.7 us
    another operation x5, other arithmetic, solve_rows(): solved = jax.scipy.linalg.solve_triangular(factor, flattened.T, lower=True)  42.6 us
    all_to_all x1, waiting for transfers between devices, sent_and_summed(): lax.all_to_all(in_blocks(array, dim, peers), axis, 0, 0, tiled=True)  37.2 us
  transfers between devices with their start and end apart: 10, of which 10 were waited for; matrix products, arithmetic and copies ran while one was open for 2% of the time, Pallas kernels for 0%

profile of v1, /device:TPU:64, one launch (start us, length us, event | category | flops | bytes accessed | tf_op | source)
XLA Modules:
  0.0 902.0 jit_solution(10951028703027102467)
XLA Ops:
  6.5 4.8 copy.55
  14.0 2.5 copy.60
  16.6 43.2 %all-gather.12.cloned.1.call-done = f32[8,256,1,256]{3,1,2,0:T(8,128)} async-done(((f32[1,256,1,256]{3,1,2,0:T(8,128)}), f32[8,256,1,256]{3,1,2,0:T(8,128)}) %all-gather.12.cloned.1.call-update) | async-done | bytes 2097168 | tf_op jit(solution)/shard_map/all_gather | solution.py:10
  61.2 11.7 %cholesky.130 = f32[128,128]{1,0:T(8,128)S(1)} custom-call(f32[128,128]{1,0:T(8,128)S(1)} %cholesky.194), custom_call_target="Cholesky" | custom-call | tf_op jit(solution)/shard_map/jit(cholesky)/cholesky | solution.py:105
  72.9 9.8 %custom-call.13 = f32[1,128,128]{1,2,0:T(8,128)S(1)} custom-call(f32[1,128,128]{2,1,0:T(8,128)S(1)} %get-tuple-element.203), custom_call_target="InvertDiagBlocksLowerTriangular" | custom-call | tf_op jit(solution)/shard_map/jit(cholesky)/cholesky | solution.py:105
  83.2 11.7 %cholesky.147 = f32[128,128]{1,0:T(8,128)S(1)} custom-call(f32[128,128]{1,0:T(8,128)S(1)} %convolution_subtract_fusion.3), custom_call_target="Cholesky" | custom-call | tf_op jit(solution)/shard_map/jit(cholesky)/cholesky | solution.py:105
  97.8 4.4 while.6
  102.8 19.7 %custom-call.14 = f32[2,128,128]{1,2,0:T(8,128)S(1)} custom-call(f32[2,128,128]{2,1,0:T(8,128)S(1)} %get-tuple-element.106), custom_call_target="InvertDiagBlocksLowerTriangular" | custom-call | tf_op jit(solution)/shard_map/jit(_solve_triangular)/triangular_solve | solution.py:46
  135.9 85.3 %all-gather.6.cloned.1.call-done = f32[8,4,256,256]{3,2,1,0:T(8,128)} async-done(((f32[1,4,256,256]{3,2,1,0:T(8,128)}), f32[8,4,256,256]{3,2,1,0:T(8,128)}) %all-gather.6.cloned.1.call-update) | async-done | bytes 8388624 | tf_op jit(solution)/shard_map/all_gather | solution.py:15
  221.1 5.1 reduce_sum.31
  229.1 1.8 copy.93
  231.9 42.3 %reduce-scatter.13.cloned.1.call-done = f32[32,256]{1,0:T(8,128)} async-done(((f32[256,256]{1,0:T(8,128)}), f32[32,256]{1,0:T(8,128)}) %reduce-scatter.13.cloned.1.call-update) | async-done | bytes 32784 | tf_op jit(solution)/shard_map/reduce_scatter | solution.py:28
  274.2 25.1 %all_gather.28 = f32[256,256]{1,0:T(8,128)S(1)} all-gather(f32[32,256]{1,0:T(8,128)} %reduce-scatter.13.cloned.1.call-done), channel_id=1, replica_groups=mesh['layer'=8,'row'=8,'col'=8] {'row'}, dimensions={0}, use_global_device_ids=true | all-gather | bytes 294912 | tf_op jit(solution)/shard_map/all_gather | solution.py:29
  299.3 16.2 %reduce-scatter.15.cloned.1.call-done = f32[32,256]{1,0:T(8,128)} async-done(((f32[256,256]{1,0:T(8,128)}), f32[32,256]{1,0:T(8,128)}) %reduce-scatter.15.cloned.1.call-update) | async-done | bytes 32784 | tf_op jit(solution)/shard_map/reduce_scatter | solution.py:28
  315.5 25.1 %all_gather.29 = f32[256,256]{1,0:T(8,128)S(1)} all-gather(f32[32,256]{1,0:T(8,128)} %reduce-scatter.15.cloned.1.call-done), channel_id=1, replica_groups=mesh['layer'=8,'row'=8,'col'=8] {'row'}, dimensions={0}, use_global_device_ids=true | all-gather | bytes 294912 | tf_op jit(solution)/shard_map/all_gather | solution.py:29
  343.4 6.5 conditional.2
  344.8 5.1 fusion
  349.9 2.3 slice.136
  352.2 2.5 copy.101
  354.8 132.0 %all-reduce.3.cloned.1.call-done = f32[4,256,256]{1,0,2:T(4,128)} async-done(((f32[4,256,256]{1,0,2:T(4,128)}), f32[4,256,256]{1,0,2:T(4,128)}) %all-reduce.3.cloned.1.call-update) | async-done | bytes 1048592 | tf_op jit(solution)/shard_map/psum | solution.py:101
  490.7 2.6 copy.70
  493.3 2.5 copy.71
  495.8 35.6 %all-gather.8.cloned.1.call-done = f32[8,256,256]{2,1,0:T(8,128)} async-done(((f32[1,256,256]{2,1,0:T(8,128)}), f32[8,256,256]{2,1,0:T(8,128)}) %all-gather.8.cloned.1.call-update) | async-done | bytes 2097168 | tf_op jit(solution)/shard_map/all_gather | solution.py:10
  531.4 1.7 dynamic_slice.30
  534.9 1.8 copy.69
  538.4 11.7 %cholesky.164 = f32[128,128]{1,0:T(8,128)S(1)} custom-call(f32[128,128]{1,0:T(8,128)S(1)} %cholesky.197), custom_call_target="Cholesky" | custom-call | tf_op jit(solution)/shard_map/jit(cholesky)/cholesky | solution.py:105
  550.1 9.8 %custom-call.15 = f32[1,128,128]{1,2,0:T(8,128)S(1)} custom-call(f32[1,128,128]{2,1,0:T(8,128)S(1)} %get-tuple-element.199), custom_call_target="InvertDiagBlocksLowerTriangular" | custom-call | tf_op jit(solution)/shard_map/jit(cholesky)/cholesky | solution.py:105
  562.1 11.7 %cholesky.181 = f32[128,128]{1,0:T(8,128)S(1)} custom-call(f32[128,128]{1,0:T(8,128)S(1)} %convolution_subtract_fusion.2), custom_call_target="Cholesky" | custom-call | tf_op jit(solution)/shard_map/jit(cholesky)/cholesky | solution.py:105
  576.6 1.7 fusion.24
  578.3 5.7 while.7
  584.7 20.5 %custom-call.16 = f32[2,128,128]{1,2,0:T(8,128)S(1)} custom-call(f32[2,128,128]{2,1,0:T(8,128)} %copy-done.7), custom_call_target="InvertDiagBlocksLowerTriangular" | custom-call | tf_op jit(solution)/shard_map/jit(_solve_triangular)/triangular_solve | solution.py:46
  610.2 2.5 copy.84
  612.8 2.4 select_select_fusion
  615.2 90.8 %all-gather.10.cloned.1.call-done = f32[8,4,256,256]{3,2,1,0:T(8,128)} async-done(((f32[1,4,256,256]{3,2,1,0:T(8,128)}), f32[8,4,256,256]{3,2,1,0:T(8,128)}) %all-gather.10.cloned.1.call-update) | async-done | bytes 8388624 | tf_op jit(solution)/shard_map/all_gather | solution.py:15
  706.0 5.1 reduce_sum.33
  711.1 2.5 copy.98
  713.6 2.8 broadcast_select_fusion.2
  716.5 1.8 copy.95
  719.2 42.4 %reduce-scatter.17.cloned.1.call-done = f32[32,256]{1,0:T(8,128)} async-done(((f32[256,256]{1,0:T(8,128)}), f32[32,256]{1,0:T(8,128)}) %reduce-scatter.17.cloned.1.call-update) | async-done | bytes 32784 | tf_op jit(solution)/shard_map/reduce_scatter | solution.py:28
  761.6 25.0 %all_gather.32 = f32[256,256]{1,0:T(8,128)S(1)} all-gather(f32[32,256]{1,0:T(8,128)} %reduce-scatter.17.cloned.1.call-done), channel_id=1, replica_groups=mesh['layer'=8,'row'=8,'col'=8] {'row'}, dimensions={0}, use_global_device_ids=true | all-gather | bytes 294912 | tf_op jit(solution)/shard_map/all_gather | solution.py:29
  786.6 16.4 %reduce-scatter.19.cloned.1.call-done = f32[32,256]{1,0:T(8,128)} async-done(((f32[256,256]{1,0:T(8,128)}), f32[32,256]{1,0:T(8,128)}) %reduce-scatter.19.cloned.1.call-update) | async-done | bytes 32784 | tf_op jit(solution)/shard_map/reduce_scatter | solution.py:28
  803.0 25.0 %all_gather.33 = f32[256,256]{1,0:T(8,128)S(1)} all-gather(f32[32,256]{1,0:T(8,128)} %reduce-scatter.19.cloned.1.call-done), channel_id=1, replica_groups=mesh['layer'=8,'row'=8,'col'=8] {'row'}, dimensions={0}, use_global_device_ids=true | all-gather | bytes 294912 | tf_op jit(solution)/shard_map/all_gather | solution.py:29
  828.8 3.2 copy.77
  832.0 14.9 %all-to-all-start = ((f32[8,4,32,2,256]{4,2,3,1,0:T(8,128)}), f32[8,4,32,2,256]{4,2,3,1,0:T(8,128)}, u32[]{:S(2)}, u32[]{:S(2)}) async-start(f32[8,4,32,2,256]{4,2,3,1,0:T(8,128)} %copy.77), calls=%async_computation | async-start | bytes 4194304 | tf_op jit(solution)/shard_map/all_to_all | solution.py:39
  848.3 2.5 fusion.21
  852.3 37.2 %all-to-all-done = f32[8,4,32,2,256]{4,2,3,1,0:T(8,128)} async-done(((f32[8,4,32,2,256]{4,2,3,1,0:T(8,128)}), f32[8,4,32,2,256]{4,2,3,1,0:T(8,128)}, u32[]{:S(2)}, u32[]{:S(2)}) %all-to-all-start) | async-done | bytes 2097184 | tf_op jit(solution)/shard_map/all_to_all | solution.py:39
  889.4 1.8 reduce_sum.35
  893.2 2.1 copy.80
  (117 shorter events, 55.7 us)
Async XLA Ops:
  6.5 53.3 %all-gather.12.cloned.1.call-start = ((), (), s32[]{:S(2)}) async-start(), calls=%async_computation.9 | async-start | bytes 2359296 | tf_op jit(solution)/shard_map/all_gather | solution.py:10
  12.4 208.7 %all-gather.6.cloned.1.call-start = ((), (), s32[]{:S(2)}) async-start(), calls=%async_computation.5 | async-start | bytes 9437184 | tf_op jit(solution)/shard_map/all_gather | solution.py:15
  102.2 0.6 copy-start.8
  126.4 2.6 copy-start.3
  130.3 144.0 %reduce-scatter.13.cloned.1.call-start = ((), (), s32[]{:S(2)}) async-start(), calls=%async_computation.10 | async-start | bytes 294912 | tf_op jit(solution)/shard_map/reduce_scatter | solution.py:28
  230.9 84.6 %reduce-scatter.15.cloned.1.call-start = ((), (), s32[]{:S(2)}) async-start(), calls=%async_computation.11 | async-start | bytes 294912 | tf_op jit(solution)/shard_map/reduce_scatter | solution.py:28
  231.9 255.0 %all-reduce.3.cloned.1.call-start = ((), (), s32[]{:S(2)}) async-start(), calls=%async_computation.6 | async-start | bytes 2097152 | tf_op jit(solution)/shard_map/psum | solution.py:101
  354.8 176.6 %all-gather.8.cloned.1.call-start = ((), (), s32[]{:S(2)}) async-start(), calls=%async_computation.7 | async-start | bytes 2359296 | tf_op jit(solution)/shard_map/all_gather | solution.py:10
  488.4 1.0 copy-start.2
  490.5 215.6 %all-gather.10.cloned.1.call-start = ((), (), s32[]{:S(2)}) async-start(), calls=%async_computation.8 | async-start | bytes 9437184 | tf_op jit(solution)/shard_map/all_gather | solution.py:15
  537.7 0.7 copy-start.6
  573.9 2.7 copy-start.5
  584.1 0.6 copy-start.7
  609.1 3.6 copy-start.4
  615.2 146.4 %reduce-scatter.17.cloned.1.call-start = ((), (), s32[]{:S(2)}) async-start(), calls=%async_computation.12 | async-start | bytes 294912 | tf_op jit(solution)/shard_map/reduce_scatter | solution.py:28
  718.2 84.7 %reduce-scatter.19.cloned.1.call-start = ((), (), s32[]{:S(2)}) async-start(), calls=%async_computation.13 | async-start | bytes 294912 | tf_op jit(solution)/shard_map/reduce_scatter | solution.py:28
  832.0 57.5 %all-to-all-start = ((f32[8,4,32,2,256]{4,2,3,1,0:T(8,128)}), f32[8,4,32,2,256]{4,2,3,1,0:T(8,128)}, u32[]{:S(2)}, u32[]{:S(2)}) async-start(f32[8,4,32,2,256]{4,2,3,1,0:T(8,128)} %copy.77), calls=%async_computation | async-start | bytes 4194304 | tf_op jit(solution)/shard_map/all_to_all | solution.py:39
  848.2 2.6 copy-start
  852.3 39.3 %copy-start.1 = (f32[4,256,2,256]{1,0,3,2:T(4,128)S(1)}, f32[4,256,2,256]{1,0,3,2:T(4,128)}, u32[]{:S(2)}) copy-start(f32[4,256,2,256]{1,0,3,2:T(4,128)} %fusion.15) | copy-start | bytes 6291460
Sparse Core Ops, SparseCore 0:
  12.5 47.2 all-gather.11
  130.4 90.6 all-gather.5
  231.1 43.1 reduce-scatter.12
  276.9 38.5 reduce-scatter.14
  354.9 131.9 all-reduce.2
  490.6 40.7 all-gather.7
  615.3 90.6 all-gather.9
  718.4 43.1 reduce-scatter.16
  764.3 38.5 reduce-scatter.18
